TPU v7x, 32 devices: a whole 2x2x4 slice. The times are simulated.
32 devices in a mesh: dp: 2 (over x), tensor: 8 (over z, y), pipe: 2 (over core).
Axes of the slice: x: 2, y: 2, z: 4, core: 2. Of those that a mesh axis runs over, the one named last changes fastest.
Arguments:
- hidden: bfloat16 [2, 1024, 7168], P('pipe', ('dp', 'tensor')), may hold values from -200 to 200
- head_table: bfloat16 [81920, 7168], P(('dp', 'tensor')), may hold values from -1 to 1
- targets: int32 [2, 1024], P('pipe', ('dp', 'tensor')), may hold values from 0 to 81919
Outputs:
- token_loss: float32 [2, 1024], P('pipe', ('dp', 'tensor'))
- mean_loss: float32 [], replicated
All inputs are finite; a program needn't handle non-finite values.
Results may differ from a plain program's by a relative error of at most 0.0003.
Values may be sent and summed in bfloat16 or wider, within the bound.
No kernel may reach another device: no remote copies, remote signals or barrier semaphores. Data moves between devices by JAX's collectives and lax.ppermute only.
A program may use at most 192 MiB of HBM per device.

v0:
```python
import jax
import jax.numpy as jnp
from jax import lax
from jax.sharding import PartitionSpec as P


def body(hidden, head_table, targets):
    row_count = head_table.shape[0]
    position = lax.axis_index(("dp", "tensor"))
    offset = position * row_count
    tokens_own = hidden[0]
    labels_own = targets[0]
    own_count = tokens_own.shape[0]
    columns = lax.broadcasted_iota(jnp.int32, (1, row_count), 1)
    gathered, labels = (
        lax.all_gather(tokens_own, ("dp", "tensor"), axis=0, tiled=True),
        lax.all_gather(labels_own, ("dp", "tensor"), axis=0, tiled=True),
    )
    logits = lax.dot_general(
        gathered, head_table, (((1,), (1,)), ((), ())), preferred_element_type=jnp.float32
    )
    local_ids = (labels - offset)[:, None]
    picked = jnp.sum(jnp.where(columns == local_ids, logits, 0.0), axis=1)
    logits, picked = (logits, picked)
    local_maxima = jnp.max(logits, axis=1)
    maxima = lax.pmax(local_maxima, ("dp", "tensor"))
    exp_sums = jnp.sum(jnp.exp(logits - maxima[:, None]), axis=1)
    totals, chosen = lax.psum((exp_sums, picked), ("dp", "tensor"))
    losses = maxima + jnp.log(totals) - chosen
    own_losses = lax.dynamic_slice_in_dim(losses, position * own_count, own_count, 0)
    loss_sum = lax.psum(jnp.sum(losses), "pipe")
    mean_loss = loss_sum / (losses.shape[0] * lax.axis_size("pipe"))
    return (own_losses[None, :], mean_loss)


def solution(mesh):
    in_specs = (
        P("pipe", ("dp", "tensor"), None),
        P(("dp", "tensor"), None),
        P("pipe", ("dp", "tensor")),
    )
    out_specs = (P("pipe", ("dp", "tensor")), P())
    return jax.shard_map(body, mesh=mesh, in_specs=in_specs, out_specs=out_specs, check_vma=False)
```

profile of v0, /device:TPU:0, one launch (start us, length us, event | category | flops | bytes accessed | tf_op | source)
XLA Modules:
  0.0 370.6 jit_solution(1653511090591210883)
XLA Ops:
  7.2 0.0 all-gather.4.cloned.1.call-start
  7.2 0.7 all-gather.4.cloned.1.call-update
  7.9 1.2 dynamic-slice
  9.8 0.8 bitcast_dynamic-update-slice_fusion
  10.6 16.3 %all-reduce = s32[1024]{0:T(1024)S(1)} all-reduce(s32[1024]{0:T(1024)S(1)} %bitcast_dynamic-update-slice_fusion), channel_id=3, replica_groups=mesh['dp'=2,'tensor'=8,'pipe'=2] {'dp','tensor'}, use_global_device_ids=true, to_apply=%add | all-reduce | flops 1024 | bytes 8192
  26.9 0.6 broadcast_subtract_fusion
  27.5 157.2 %all-gather.4.cloned.1.call-done = bf16[1,1024,7168]{2,1,0:T(8,128)(2,1)} async-done(((bf16[1,64,7168]{2,1,0:T(8,128)(2,1)}), bf16[1,1024,7168]{2,1,0:T(8,128)(2,1)}) %all-gather.4.cloned.1.call-update) | async-done | bytes 14680080 | tf_op jit(solution)/shard_map/all_gather | solution.py:16
  184.7 0.0 copy-start
  184.7 86.9 %fusion.3 = (f32[1024]{0:T(1024)S(1)}, f32[1024,5120]{1,0:T(8,128)}) fusion(bf16[5120,7168]{1,0:T(8,128)(2,1)} %param.4, bf16[1,1024,7168]{2,1,0:T(8,128)(2,1)} %all-gather.4.cloned.1.call-done), kind=kOutput, calls=%fused_computation.10 | convolution fusion | flops 75167170560 | bytes 109056000 | tf_op jit(solution)/shard_map/dot_general | solution.py:19
  271.7 38.8 %pmax.7 = f32[1024]{0:T(1024)S(1)} all-reduce(f32[1024]{0:T(1024)S(1)} %get-tuple-element.8), channel_id=1, replica_groups=mesh['dp'=2,'tensor'=8,'pipe'=2] {'dp','tensor'}, use_global_device_ids=true, to_apply=%region_1.2 | all-reduce | flops 1024 | bytes 8192 | tf_op jit(solution)/shard_map/pmax | solution.py:26
  310.5 0.0 copy-done
  310.5 10.1 %exponential_reduce_fusion = (f32[1024]{0:T(1024)S(1)}, f32[1024]{0:T(1024)S(1)}) fusion(f32[1024,5120]{1,0:T(8,128)} %get-tuple-element.9, f32[1024]{0:T(1024)S(1)} %pmax.7, s32[1024]{0:T(1024)S(1)} %copy-done), kind=kLoop, calls=%fused_computation.2 | loop fusion | flops 26212352 | bytes 20987904 | tf_op jit(solution)/shard_map/reduce_sum | solution.py:27
  320.6 37.1 %all-reduce.1 = (f32[1024]{0:T(1024)S(1)}, f32[1024]{0:T(1024)S(1)}) all-reduce(f32[1024]{0:T(1024)S(1)} %get-tuple-element.3, f32[1024]{0:T(1024)S(1)} %get-tuple-element.2), channel_id=1, replica_groups=mesh['dp'=2,'tensor'=8,'pipe'=2] {'dp','tensor'}, use_global_device_ids=true, to_apply=%region_5.6 | all-reduce | flops 2048 | bytes 16384 | tf_op jit(solution)/shard_map/psum | solution.py:28
  357.7 0.6 fusion.2
  358.3 3.1 psum.23
  361.4 0.6 dynamic-slice_bitcast_fusion
  (1 shorter events, 0.0 us)
Async XLA Ops:
  7.2 177.5 %all-gather.4.cloned.1.call-start = ((), (), s32[]{:S(2)}) async-start(), calls=%async_computation | async-start | bytes 15597568 | tf_op jit(solution)/shard_map/all_gather | solution.py:16
  184.7 125.8 %copy-start = (s32[1024]{0:T(1024)S(1)}, s32[1024]{0:T(1024)}, u32[]{:S(2)}) copy-start(s32[1024]{0:T(1024)} %broadcast_subtract_fusion) | copy-start | bytes 12292
Sparse Core Ops, SparseCore 0:
  10.7 173.9 all-gather.3
where the time goes:
time: 371 us
  waiting for transfers between devices  158 us (43%)
  blocking collectives  95.3 us (26%)
  matrix products  86.9 us (23%)
  between operations  16.5 us (4%)
  other arithmetic  11.3 us (3%)
    all_gather x1, waiting for transfers between devices, body(): lax.all_gather(tokens_own, ('dp', 'tensor'), axis=0, tiled=True)  157 us
    dot_general x1, matrix products, body(): lax.dot_general(gathered, head_table, (((1,), (1,)), ((), ())), preferred...  86.9 us
    pmax x1, blocking collectives, body(): maxima = lax.pmax(local_maxima, ('dp', 'tensor'))  38.8 us
    psum x1, blocking collectives, body(): totals, chosen = lax.psum((exp_sums, picked), ('dp', 'tensor'))  37.1 us
    unnamed x1, blocking collectives  16.3 us
    reduce_sum x1, other arithmetic, body(): exp_sums = jnp.sum(jnp.exp(logits - maxima[:, None]), axis=1)  10.1 us
  transfers between devices with their start and end apart: 1, of which 1 were waited for; matrix products, arithmetic and copies ran while one was open for 1% of the time, Pallas kernels for 0%

commit v1 on v0

--- a/solution.py
+++ b/solution.py
@@ -1,7 +1,15 @@
+import functools
 import jax
 import jax.numpy as jnp
 from jax import lax
 from jax.sharding import PartitionSpec as P
+
+
+def connect_kinds(xx, axis_id, named_axis):
+    return jax.lax.psum(jax.lax.psum(xx, axis_name=axis_id), axis_name=named_axis)
+
+
+fill_vectors = functools.partial(connect_kinds, axis_id="tensor", named_axis="dp")
 
 
 def body(hidden, head_table, targets):
@@ -25,7 +33,7 @@
     local_maxima = jnp.max(logits, axis=1)
     maxima = lax.pmax(local_maxima, ("dp", "tensor"))
     exp_sums = jnp.sum(jnp.exp(logits - maxima[:, None]), axis=1)
-    totals, chosen = lax.psum((exp_sums, picked), ("dp", "tensor"))
+    totals, chosen = fill_vectors((exp_sums, picked))
     losses = maxima + jnp.log(totals) - chosen
     own_losses = lax.dynamic_slice_in_dim(losses, position * own_count, own_count, 0)
     loss_sum = lax.psum(jnp.sum(losses), "pipe")

time: 371 us -> 356 us (0.960)
  blocking collectives: 95.3 us -> 80.6 us
    psum x1 -> x2, blocking collectives: 37.1 us -> 22.4 us  [the longest x1 17.4 us: connect_kinds(): jax.lax.psum(xx, axis_name=axis_id)]
where the time goes in v1:
time: 356 us
  waiting for transfers between devices  158 us (44%)
  matrix products  86.9 us (24%)
  blocking collectives  80.6 us (23%)
  between operations  16.5 us (5%)
  other arithmetic  11.3 us (3%)
    all_gather x1, waiting for transfers between devices, body(): lax.all_gather(tokens_own, ('dp', 'tensor'), axis=0, tiled=True)  157 us
    dot_general x1, matrix products, body(): lax.dot_general(gathered, head_table, (((1,), (1,)), ((), ())), preferred...  86.9 us
    pmax x1, blocking collectives, body(): maxima = lax.pmax(local_maxima, ('dp', 'tensor'))  38.8 us
    psum x1, blocking collectives, connect_kinds(): jax.lax.psum(xx, axis_name=axis_id)  17.4 us
    unnamed x1, blocking collectives  16.3 us
    reduce_sum x1, other arithmetic, body(): exp_sums = jnp.sum(jnp.exp(logits - maxima[:, None]), axis=1)  10.1 us
  transfers between devices with their start and end apart: 1, of which 1 were waited for; matrix products, arithmetic and copies ran while one was open for 1% of the time, Pallas kernels for 0%

profile of v1, /device:TPU:0, one launch (start us, length us, event | category | flops | bytes accessed | tf_op | source)
XLA Modules:
  0.0 355.9 jit_solution(15578580453674048867)
XLA Ops:
  7.2 0.0 all-gather.4.cloned.1.call-start
  7.2 0.7 all-gather.4.cloned.1.call-update
  7.9 1.2 dynamic-slice
  9.8 0.8 bitcast_dynamic-update-slice_fusion
  10.6 16.3 %all-reduce = s32[1024]{0:T(1024)S(1)} all-reduce(s32[1024]{0:T(1024)S(1)} %bitcast_dynamic-update-slice_fusion), channel_id=3, replica_groups=mesh['dp'=2,'tensor'=8,'pipe'=2] {'dp','tensor'}, use_global_device_ids=true, to_apply=%add | all-reduce | flops 1024 | bytes 8192
  26.9 0.6 broadcast_subtract_fusion
  27.5 157.2 %all-gather.4.cloned.1.call-done = bf16[1,1024,7168]{2,1,0:T(8,128)(2,1)} async-done(((bf16[1,64,7168]{2,1,0:T(8,128)(2,1)}), bf16[1,1024,7168]{2,1,0:T(8,128)(2,1)}) %all-gather.4.cloned.1.call-update) | async-done | bytes 14680080 | tf_op jit(solution)/shard_map/all_gather | solution.py:24
  184.7 0.0 copy-start
  184.7 86.9 %fusion.3 = (f32[1024]{0:T(1024)S(1)}, f32[1024,5120]{1,0:T(8,128)}) fusion(bf16[5120,7168]{1,0:T(8,128)(2,1)} %param.4, bf16[1,1024,7168]{2,1,0:T(8,128)(2,1)} %all-gather.4.cloned.1.call-done), kind=kOutput, calls=%fused_computation.10 | convolution fusion | flops 75167170560 | bytes 109056000 | tf_op jit(solution)/shard_map/dot_general | solution.py:27
  271.7 38.8 %pmax.7 = f32[1024]{0:T(1024)S(1)} all-reduce(f32[1024]{0:T(1024)S(1)} %get-tuple-element.10), channel_id=1, replica_groups=mesh['dp'=2,'tensor'=8,'pipe'=2] {'dp','tensor'}, use_global_device_ids=true, to_apply=%region_1.2 | all-reduce | flops 1024 | bytes 8192 | tf_op jit(solution)/shard_map/pmax | solution.py:34
  310.5 0.0 copy-done
  310.5 10.1 %exponential_reduce_fusion = (f32[1024]{0:T(1024)S(1)}, f32[1024]{0:T(1024)S(1)}) fusion(f32[1024,5120]{1,0:T(8,128)} %get-tuple-element.11, f32[1024]{0:T(1024)S(1)} %pmax.7, s32[1024]{0:T(1024)S(1)} %copy-done), kind=kLoop, calls=%fused_computation.2 | loop fusion | flops 26212352 | bytes 20987904 | tf_op jit(solution)/shard_map/reduce_sum | solution.py:35
  320.6 17.4 %all-reduce.1 = (f32[1024]{0:T(1024)S(1)}, f32[1024]{0:T(1024)S(1)}) all-reduce(f32[1024]{0:T(1024)S(1)} %get-tuple-element.3, f32[1024]{0:T(1024)S(1)} %get-tuple-element.2), channel_id=1, replica_groups=mesh['dp'=2,'tensor'=8,'pipe'=2] {'tensor'}, use_global_device_ids=true, to_apply=%region_6.7 | all-reduce | flops 2048 | bytes 16384 | tf_op jit(solution)/shard_map/psum | solution.py:9
  338.0 5.0 %all-reduce.2 = (f32[1024]{0:T(1024)S(1)}, f32[1024]{0:T(1024)S(1)}) all-reduce(f32[1024]{0:T(1024)S(1)} %get-tuple-element.4, f32[1024]{0:T(1024)S(1)} %get-tuple-element.5), channel_id=1, replica_groups=mesh['dp'=2,'tensor'=8,'pipe'=2] {'dp'}, use_global_device_ids=true, to_apply=%region_7.8 | all-reduce | flops 2048 | bytes 16384 | tf_op jit(solution)/shard_map/psum | solution.py:9
  343.0 0.6 fusion.2
  343.6 3.1 psum.39
  346.7 0.6 dynamic-slice_bitcast_fusion
  (1 shorter events, 0.0 us)
Async XLA Ops:
  7.2 177.5 %all-gather.4.cloned.1.call-start = ((), (), s32[]{:S(2)}) async-start(), calls=%async_computation | async-start | bytes 15597568 | tf_op jit(solution)/shard_map/all_gather | solution.py:24
  184.7 125.8 %copy-start = (s32[1024]{0:T(1024)S(1)}, s32[1024]{0:T(1024)}, u32[]{:S(2)}) copy-start(s32[1024]{0:T(1024)} %broadcast_subtract_fusion) | copy-start | bytes 12292
Sparse Core Ops, SparseCore 0:
  10.7 173.9 all-gather.3
